TPU v7x, 512 devices: a whole 4x4x16 slice. The times are simulated.
512 devices in a mesh: chan: 64 (over y, x, z_hi, core), freq: 8 (over z_lo).
Axes of the slice: x: 4, y: 4, z: 16 (z_hi: 2, z_lo: 8; z = z_hi * 8 + z_lo), core: 2. Of those that a mesh axis runs over, the one named last changes fastest.
Arguments:
- spectra: bfloat16 [256, 2, 16, 8192], P('freq', None, None, 'chan'), may hold values from -20 to 20
- model: bfloat16 [256, 2, 8, 8192], P('freq', None, None, 'chan'), may hold values from -6 to 6
- channel_ok: int32 [8192], replicated, may hold values 0 or 1
- limits: int32 [64], replicated, may hold values from 128 to 1024, as said below
Outputs:
- adjoint: float32 [256, 2, 16, 8192], P('freq', None, None, 'chan')
- misfit: float32 [], replicated
Inputs may be any that keep to these rules, and one draw needn't show every extreme that they name: `limits`: one block has the limit 128 and another the limit 1024.
All inputs are finite; a program needn't handle non-finite values.
Results may differ from a plain program's by a relative error of at most 0.00053.
Values may be sent and summed in bfloat16 or wider, within the bound.
A program may use at most 64 MiB of HBM per device.

v0:
```python
import jax
import jax.numpy as jnp
from jax import lax
from jax.sharding import PartitionSpec as P

F = 256
W = 16
BAND = 1024
GROUP = 4


def permute(x, pairs):
    return lax.ppermute(x, "chan", pairs)


def shift_pairs(peers, by):
    return [(i, (i + by) % peers) for i in range(peers)]


def group_pairs(peers, t):
    return [(i, i // GROUP * GROUP + (i % GROUP + t) % GROUP) for i in range(peers)]


def exchange(chunks, j, peers):
    rel = jnp.roll(chunks, -j, axis=0)
    got = [rel[0]] + [permute(rel[t], group_pairs(peers, t)) for t in range(1, GROUP)]
    got = jnp.stack(got, axis=0)
    order = (j - jnp.arange(GROUP)) % GROUP
    return jnp.take(got, order, axis=0)


def pair_terms(first, second, ok_first, ok_second, limit_first, shift_blocks):
    row_count = first.shape[2]
    block_width = first.shape[4]
    row_scale = jnp.concatenate(
        [jnp.full((W,), 1.0 / W, jnp.float32), jnp.full((row_count - W,), -1.0, jnp.float32)]
    ).astype(jnp.bfloat16)
    scaled = first * row_scale[None, None, :, None, None]
    fb = first.shape[0]
    nb = first.shape[3]
    stacked_left = jnp.stack(
        [
            scaled.reshape(fb, 2 * row_count, nb, block_width),
            jnp.concatenate([scaled[:, 1], -scaled[:, 0]], axis=1),
        ],
        axis=0,
    )
    right_rows = second.reshape(fb, 2 * row_count, nb, block_width)
    cross_spec = jnp.einsum(
        "xfrbc,frbd->xfbcd", stacked_left, right_rows, preferred_element_type=jnp.float32
    )
    row_index = lax.broadcasted_iota(jnp.int32, (block_width, block_width), 0)
    col_index = lax.broadcasted_iota(jnp.int32, (block_width, block_width), 1)
    offset = shift_blocks * block_width + col_index - row_index
    inside = ((offset[None] >= 1) & (offset[None] <= limit_first[:, None, None])).astype(
        jnp.float32
    )
    live_mask = ok_first[:, :, None] * ok_second[:, None, :] * inside
    residual = cross_spec * live_mask[None, None]
    piece_loss = 0.5 * jnp.sum(residual * residual)
    rounded = residual.astype(jnp.bfloat16)
    far_spec = second[:, :, :W].reshape(fb, 2 * W, nb, block_width)
    near_spec = first[:, :, :W].reshape(fb, 2 * W, nb, block_width)
    toward = jnp.einsum("xfbcd,fvbd->xfvbc", rounded, far_spec, preferred_element_type=jnp.float32)
    first_real = toward[0, :, :W] - toward[1, :, W:]
    first_imag = toward[0, :, W:] + toward[1, :, :W]
    backward = jnp.einsum(
        "xfbcd,fvbc->xfvbd", rounded, near_spec, preferred_element_type=jnp.float32
    )
    second_real = backward[0, :, :W] + backward[1, :, W:]
    second_imag = backward[0, :, W:] - backward[1, :, :W]
    return (
        piece_loss,
        jnp.stack([first_real, first_imag], axis=1),
        jnp.stack([second_real, second_imag], axis=1),
    )


def shards(spectra, model, channel_ok, limits):
    payload = jnp.concatenate([spectra, model], axis=2)
    fl, _, rows, bw = payload.shape
    peers = lax.axis_size("chan")
    me = lax.axis_index("chan")
    j = me % GROUP
    column = me // GROUP
    sub = fl // GROUP
    band_blocks = BAND // bw
    halo_cols = -(-band_blocks // GROUP)
    span = GROUP * bw
    chunks = payload.reshape(GROUP, sub, 2, rows, bw)
    mine = exchange(chunks, j, peers)
    own = jnp.transpose(mine, (1, 2, 3, 0, 4)).reshape(sub, 2, rows, span)
    parts = [own] + [permute(own, shift_pairs(peers, -GROUP * h)) for h in range(1, halo_cols + 1)]
    ext = jnp.concatenate(parts, axis=3)
    total = ext.shape[3]
    ok_all = channel_ok.astype(jnp.float32)
    ok_wide = jnp.concatenate([ok_all, ok_all[:total]])
    ok_ext = lax.dynamic_slice_in_dim(ok_wide, column * span, total)
    lim = lax.dynamic_slice_in_dim(limits, column * GROUP, GROUP)
    first = ext[:, :, :, :span].reshape(sub, 2, rows, GROUP, bw)
    ok_first = ok_ext[:span].reshape(GROUP, bw)
    misfit_sum = jnp.zeros((), jnp.float32)
    near_acc = jnp.zeros((sub, 2, W, GROUP, bw), jnp.float32)
    far_acc = jnp.zeros((sub, 2, W, total), jnp.float32)
    for s in range(band_blocks + 1):
        second = ext[:, :, :, s * bw : s * bw + span].reshape(sub, 2, rows, GROUP, bw)
        ok_second = ok_ext[s * bw : s * bw + span].reshape(GROUP, bw)
        piece_loss, near_terms, far_terms = pair_terms(first, second, ok_first, ok_second, lim, s)
        misfit_sum = misfit_sum + piece_loss
        near_acc = near_acc + near_terms
        far_flat = far_terms.reshape(sub, 2, W, span)
        far_acc = far_acc + jnp.pad(
            far_flat, ((0, 0), (0, 0), (0, 0), (s * bw, total - span - s * bw))
        )
    adj = near_acc.reshape(sub, 2, W, span) + far_acc[:, :, :, :span]
    for h in range(1, halo_cols + 1):
        adj = adj + permute(
            far_acc[:, :, :, h * span : (h + 1) * span], shift_pairs(peers, GROUP * h)
        )
    adj = adj * (1.0 / W)
    blocks = jnp.transpose(adj.reshape(sub, 2, W, GROUP, bw), (3, 0, 1, 2, 4))
    back = exchange(blocks, j, peers)
    adjoint = back.reshape(fl, 2, W, bw)
    misfit_total = lax.psum(misfit_sum, ("chan", "freq"))
    misfit = misfit_total / float(F * bw * peers * BAND)
    return (adjoint, misfit)


def solution(mesh):
    return jax.shard_map(
        shards,
        mesh=mesh,
        in_specs=(P("freq", None, None, "chan"), P("freq", None, None, "chan"), P(), P()),
        out_specs=(P("freq", None, None, "chan"), P()),
        check_vma=False,
    )
```

profile of v0, /device:TPU:1, one launch (start us, length us, event | category | flops | bytes accessed | tf_op | source)
XLA Modules:
  0.0 330.2 jit_solution(5131253265094476053)
XLA Ops:
  0.7 1.1 pad_maximum_fusion.2
  2.6 16.3 %collective-permute-start.1 = (bf16[8,2,24,128]{3,2,1,0:T(8,128)(2,1)}, bf16[8,2,24,128]{3,2,1,0:T(8,128)(2,1)S(1)}, u32[]{:S(2)}, u32[]{:S(2)}) collective-permute-start(bf16[8,2,24,128]{3,2,1,0:T(8,128)(2,1)} %get-tuple-element.57), channel_id=1, source_target_pairs={{0,16},{8,24},{16,0},{24,8},{32,48},{40,56},{48,32},{56,40},{64,80... | collective-permute-start | bytes 294920 | tf_op jit(solution)/shard_map/ppermute | solution.py:13
  18.9 4.8 %collective-permute-start = (bf16[8,2,24,128]{3,2,1,0:T(8,128)(2,1)S(1)}, bf16[8,2,24,128]{3,2,1,0:T(8,128)(2,1)S(1)}, u32[]{:S(2)}, u32[]{:S(2)}) collective-permute-start(bf16[8,2,24,128]{3,2,1,0:T(8,128)(2,1)S(1)} %get-tuple-element.58), channel_id=1, source_target_pairs={{0,8},{8,16},{16,24},{24,0},{32,40},{40,48},{48,56},{56,32},{64,72... | collective-permute-start | bytes 294920 | tf_op jit(solution)/shard_map/ppermute | solution.py:13
  23.6 1.9 collective-permute-start.2
  28.4 1.2 multiply_select_fusion.8
  29.6 9.8 %collective-permute-done.2 = bf16[8,2,24,128]{3,2,1,0:T(8,128)(2,1)} collective-permute-done((bf16[8,2,24,128]{3,2,1,0:T(8,128)(2,1)S(1)}, bf16[8,2,24,128]{3,2,1,0:T(8,128)(2,1)}, u32[]{:S(2)}, u32[]{:S(2)}) %collective-permute-start.2) | collective-permute-done | bytes 98336 | tf_op jit(solution)/shard_map/ppermute | solution.py:13
  40.3 1.5 gather_fusion
  41.8 1.1 broadcast_multiply_fusion
  45.5 1.9 reshape.1311
  47.4 7.6 %collective-permute-start.4 = (bf16[8,2,24,512]{3,2,1,0:T(8,128)(2,1)}, bf16[8,2,24,512]{3,2,1,0:T(8,128)(2,1)S(1)}, u32[]{:S(2)}, u32[]{:S(2)}) collective-permute-start(bf16[8,2,24,512]{3,2,1,0:T(8,128)(2,1)} %reshape.1311), channel_id=1, source_target_pairs={{0,448},{8,456},{16,464},{24,472},{32,480},{40,488},{48,496},{56,5... | collective-permute-start | bytes 1179656 | tf_op jit(solution)/shard_map/ppermute | solution.py:13
  55.0 3.2 collective-permute-start.3
  58.3 1.1 maximum_bitcast_fusion
  59.4 2.9 multiply_reduce_fusion.8
  68.1 4.6 %collective-permute-done.3 = bf16[8,2,24,512]{3,2,1,0:T(8,128)(2,1)S(1)} collective-permute-done((bf16[8,2,24,512]{3,2,1,0:T(8,128)(2,1)}, bf16[8,2,24,512]{3,2,1,0:T(8,128)(2,1)S(1)}, u32[]{:S(2)}, u32[]{:S(2)}) %collective-permute-start.3) | collective-permute-done | bytes 393248 | tf_op jit(solution)/shard_map/ppermute | solution.py:13
  73.6 1.1 fusion.71
  75.6 1.8 reshape_reshape.24
  77.4 1.8 reshape.1312
  79.2 1.8 reshape_reshape.26
  81.1 1.8 reshape.1316
  84.6 2.3 fusion.72
  88.5 1.9 reshape.1320
  90.4 1.9 reshape_reshape.30
  92.3 1.9 reshape.1324
  94.1 1.8 reshape_reshape.29
  96.0 1.8 reshape.1322
  98.6 1.0 slice.638
  100.4 1.8 reshape.1318
  102.3 1.1 slice.611
  104.2 1.0 slice.591
  108.5 1.9 multiply_reduce_fusion.6
  115.1 2.0 multiply_reduce_fusion.5
  122.7 3.0 multiply_reduce_fusion.4
  129.2 1.9 multiply_reduce_fusion.3
  135.2 1.9 multiply_reduce_fusion.2
  142.0 1.9 multiply_reduce_fusion.1
  148.8 1.9 multiply_reduce_fusion.7
  154.5 1.9 multiply_reduce_fusion
  158.9 4.2 %fusion.9 = f32[8,2,16,1536]{3,1,2,0:T(2,128)S(1)} fusion(f32[8,1,16,512]{3,1,2,0:T(1,128)S(1)} %bitcast.366, f32[8,1,16,512]{3,1,2,0:T(1,128)S(1)} %bitcast.364, f32[8,1,16,512]{3,1,2,0:T(1,128)S(1)} %bitcast.360, f32[8,1,16,512]{3,1,2,0:T(1,128)S(1)} %bitcast.359, f32[8,1,16,512]{3,1,2,0:T(1,128)S(1)} %bitcast.357, f32[8,1,16,512]{3,1,2,0:T(1,128)S(1)} %bitcast.356, ...), kind=kLoop, calls=%fused_computation.37 | loop fusion | flops 22806528 | bytes 6291456 | tf_op jit(solution)/shard_map/add | solution.py:112
  163.7 1.9 collective-permute-start.5
  165.6 4.7 %collective-permute-start.6 = (f32[8,2,16,512]{3,1,2,0:T(2,128)S(1)}, f32[8,2,16,512]{3,1,2,0:T(2,128)S(1)}, u32[]{:S(2)}, u32[]{:S(2)}) collective-permute-start(f32[8,2,16,512]{3,1,2,0:T(2,128)S(1)} %get-tuple-element.5), channel_id=1, source_target_pairs={{0,64},{8,72},{16,80},{24,88},{32,96},{40,104},{48,112},{56,120},{... | collective-permute-start | bytes 1572872 | tf_op jit(solution)/shard_map/ppermute | solution.py:13
  171.3 10.8 %collective-permute-done.5 = f32[8,2,16,512]{3,1,2,0:T(2,128)S(1)} collective-permute-done((f32[8,2,16,512]{3,1,2,0:T(2,128)S(1)}, f32[8,2,16,512]{3,1,2,0:T(2,128)S(1)}, u32[]{:S(2)}, u32[]{:S(2)}) %collective-permute-start.5) | collective-permute-done | bytes 524320 | tf_op jit(solution)/shard_map/ppermute | solution.py:13
  182.1 12.8 %collective-permute-done.6 = f32[8,2,16,512]{3,1,2,0:T(2,128)S(1)} collective-permute-done((f32[8,2,16,512]{3,1,2,0:T(2,128)S(1)}, f32[8,2,16,512]{3,1,2,0:T(2,128)S(1)}, u32[]{:S(2)}, u32[]{:S(2)}) %collective-permute-start.6) | collective-permute-done | bytes 524320 | tf_op jit(solution)/shard_map/ppermute | solution.py:13
  195.0 4.5 %fusion.38 = f32[8,2,16,512]{3,1,2,0:T(2,128)S(1)} fusion(f32[8,2,16,512]{3,1,2,0:T(2,128)S(1)} %collective-permute-done.6, f32[8,2,16,512]{3,1,2,0:T(2,128)S(1)} %collective-permute-done.5, f32[8,2,16,1536]{3,1,2,0:T(2,128)S(1)} %fusion.9, f32[8,1,16,512]{3,1,2,0:T(1,128)S(1)} %bitcast.380, f32[8,1,16,512]{3,1,2,0:T(1,128)S(1)} %bitcast.379, ...), kind=kLoop, calls=%fused_computation.80 | loop fusion | flops 2752512 | bytes 6815744 | tf_op jit(solution)/shard_map/mul | solution.py:120
  200.8 3.2 collective-permute-start.9
  204.1 1.9 collective-permute-start.8
  206.0 12.3 %collective-permute-start.7 = (f32[8,2,16,128]{3,1,2,0:T(2,128)S(1)}, f32[8,2,16,128]{3,1,2,0:T(2,128)S(1)}, u32[]{:S(2)}, u32[]{:S(2)}) collective-permute-start(f32[8,2,16,128]{3,1,2,0:T(2,128)S(1)} %bitcast.386), channel_id=1, source_target_pairs={{0,8},{8,16},{16,24},{24,0},{32,40},{40,48},{48,56},{56,32},{64,72... | collective-permute-start | bytes 393224 | tf_op jit(solution)/shard_map/ppermute | solution.py:13
  224.0 101.7 %psum.7 = f32[]{:T(128)} all-reduce(f32[]{:T(128)S(6)} %add.589), channel_id=1, replica_groups=mesh['chan'=64,'freq'=8] {'chan','freq'}, use_global_device_ids=true, to_apply=%region_9.10 | all-reduce | flops 1 | bytes 8 | tf_op jit(solution)/shard_map/psum | solution.py:124
  326.7 1.2 gather_fusion.1
  (243 shorter events, 61.3 us)
Async XLA Ops:
  0.6 26.7 %copy-start.45 = (s32[8192]{0:T(1024)S(1)}, s32[8192]{0:T(1024)}, u32[]{:S(2)}) copy-start(s32[8192]{0:T(1024)} %param.6) | copy-start | bytes 98308
  0.6 27.3 %copy-start.46 = (s32[64]{0:T(128)S(1)}, s32[64]{0:T(128)}, u32[]{:S(2)}) copy-start(s32[64]{0:T(128)} %param.7) | copy-start | bytes 772
  2.6 26.9 %collective-permute-start.1 = (bf16[8,2,24,128]{3,2,1,0:T(8,128)(2,1)}, bf16[8,2,24,128]{3,2,1,0:T(8,128)(2,1)S(1)}, u32[]{:S(2)}, u32[]{:S(2)}) collective-permute-start(bf16[8,2,24,128]{3,2,1,0:T(8,128)(2,1)} %get-tuple-element.57), channel_id=1, source_target_pairs={{0,16},{8,24},{16,0},{24,8},{32,48},{40,56},{48,32},{56,40},{64,80... | collective-permute-start | bytes 294920 | tf_op jit(solution)/shard_map/ppermute | solution.py:13
  18.9 10.7 %collective-permute-start = (bf16[8,2,24,128]{3,2,1,0:T(8,128)(2,1)S(1)}, bf16[8,2,24,128]{3,2,1,0:T(8,128)(2,1)S(1)}, u32[]{:S(2)}, u32[]{:S(2)}) collective-permute-start(bf16[8,2,24,128]{3,2,1,0:T(8,128)(2,1)S(1)} %get-tuple-element.58), channel_id=1, source_target_pairs={{0,8},{8,16},{16,24},{24,0},{32,40},{40,48},{48,56},{56,32},{64,72... | collective-permute-start | bytes 294920 | tf_op jit(solution)/shard_map/ppermute | solution.py:13
  23.6 15.7 %collective-permute-start.2 = (bf16[8,2,24,128]{3,2,1,0:T(8,128)(2,1)S(1)}, bf16[8,2,24,128]{3,2,1,0:T(8,128)(2,1)}, u32[]{:S(2)}, u32[]{:S(2)}) collective-permute-start(bf16[8,2,24,128]{3,2,1,0:T(8,128)(2,1)S(1)} %get-tuple-element.59), channel_id=1, source_target_pairs={{0,24},{8,0},{16,8},{24,16},{32,56},{40,32},{48,40},{56,48},{64,88... | collective-permute-start | bytes 294920 | tf_op jit(solution)/shard_map/ppermute | solution.py:13
  47.4 25.4 %collective-permute-start.4 = (bf16[8,2,24,512]{3,2,1,0:T(8,128)(2,1)}, bf16[8,2,24,512]{3,2,1,0:T(8,128)(2,1)S(1)}, u32[]{:S(2)}, u32[]{:S(2)}) collective-permute-start(bf16[8,2,24,512]{3,2,1,0:T(8,128)(2,1)} %reshape.1311), channel_id=1, source_target_pairs={{0,448},{8,456},{16,464},{24,472},{32,480},{40,488},{48,496},{56,5... | collective-permute-start | bytes 1179656 | tf_op jit(solution)/shard_map/ppermute | solution.py:13
  55.0 17.7 %collective-permute-start.3 = (bf16[8,2,24,512]{3,2,1,0:T(8,128)(2,1)}, bf16[8,2,24,512]{3,2,1,0:T(8,128)(2,1)S(1)}, u32[]{:S(2)}, u32[]{:S(2)}) collective-permute-start(bf16[8,2,24,512]{3,2,1,0:T(8,128)(2,1)} %reshape.1311), channel_id=1, source_target_pairs={{0,480},{8,488},{16,496},{24,504},{32,0},{40,8},{48,16},{56,24},{6... | collective-permute-start | bytes 1179656 | tf_op jit(solution)/shard_map/ppermute | solution.py:13
  72.7 1.9 copy-start.3
  88.5 9.3 %copy-start.1 = (bf16[8,2,24,512]{3,2,1,0:T(8,128)(2,1)S(1)}, bf16[8,2,24,512]{3,2,1,0:T(8,128)(2,1)}, u32[]{:S(2)}) copy-start(bf16[8,2,24,512]{3,2,1,0:T(8,128)(2,1)} %copy-done) | copy-start | bytes 1179652
  102.3 3.7 %slice-start.1 = ((bf16[8,2,24,4,128]{4,3,2,1,0:T(4,128)(2,1)}), bf16[8,2,16,4,128]{4,3,2,1,0:T(4,128)(2,1)S(1)}, s32[]{:S(2)}) async-start(bf16[8,2,24,4,128]{4,3,2,1,0:T(4,128)(2,1)} %reshape.1316), calls=%async_computation.1 | async-start | bytes 524288 | tf_op jit(solution)/shard_map/slice | solution.py:62
  102.3 3.8 %slice-start = ((bf16[8,2,24,4,128]{4,3,2,1,0:T(4,128)(2,1)}), bf16[8,2,16,4,128]{4,3,2,1,0:T(4,128)(2,1)S(1)}, s32[]{:S(2)}) async-start(bf16[8,2,24,4,128]{4,3,2,1,0:T(4,128)(2,1)} %reshape.1314), calls=%async_computation | async-start | bytes 524288 | tf_op jit(solution)/shard_map/slice | solution.py:62
  103.4 2.7 slice-start.4
  105.2 1.7 slice-start.2
  106.0 1.6 slice-start.3
  106.1 2.4 copy-start.11
  111.8 3.3 %copy-start.10 = (bf16[8,48,4,128]{3,2,1,0:T(4,128)(2,1)S(1)}, bf16[8,48,4,128]{3,2,1,0:T(4,128)(2,1)}, u32[]{:S(2)}) copy-start(bf16[8,48,4,128]{3,2,1,0:T(4,128)(2,1)} %reshape_reshape.26) | copy-start | bytes 1179652
  118.5 3.3 %copy-start.4 = (bf16[8,2,24,512]{3,2,1,0:T(8,128)(2,1)S(1)}, bf16[8,2,24,512]{3,2,1,0:T(8,128)(2,1)}, u32[]{:S(2)}) copy-start(bf16[8,2,24,512]{3,2,1,0:T(8,128)(2,1)} %copy-done.3) | copy-start | bytes 1179652
  127.2 1.9 copy-start.9
  132.6 2.6 copy-start.8
  138.7 3.4 %copy-start.7 = (bf16[8,48,4,128]{3,2,1,0:T(4,128)(2,1)S(1)}, bf16[8,48,4,128]{3,2,1,0:T(4,128)(2,1)}, u32[]{:S(2)}) copy-start(bf16[8,48,4,128]{3,2,1,0:T(4,128)(2,1)} %reshape_reshape.30) | copy-start | bytes 1179652
  145.5 3.3 %copy-start.6 = (bf16[8,48,4,128]{3,2,1,0:T(4,128)(2,1)S(1)}, bf16[8,48,4,128]{3,2,1,0:T(4,128)(2,1)}, u32[]{:S(2)}) copy-start(bf16[8,48,4,128]{3,2,1,0:T(4,128)(2,1)} %reshape_reshape.24) | copy-start | bytes 1179652
  157.3 1.3 copy-start.19
  157.3 1.4 copy-start.22
  157.3 1.5 copy-start.24
  157.3 1.5 copy-start.25
  157.4 1.6 copy-start.27
  163.1 7.2 %copy-start.14 = (bf16[8,2,16,4,128]{4,2,1,3,0:T(8,128)(2,1)S(1)}, bf16[8,2,16,4,128]{4,2,1,3,0:T(8,128)(2,1)}, u32[]{:S(2)}) copy-start(bf16[8,2,16,4,128]{4,2,1,3,0:T(8,128)(2,1)} %copy.71) | copy-start | bytes 786436
  163.7 18.4 %collective-permute-start.5 = (f32[8,2,16,512]{3,1,2,0:T(2,128)S(1)}, f32[8,2,16,512]{3,1,2,0:T(2,128)S(1)}, u32[]{:S(2)}, u32[]{:S(2)}) collective-permute-start(f32[8,2,16,512]{3,1,2,0:T(2,128)S(1)} %get-tuple-element.4), channel_id=1, source_target_pairs={{0,32},{8,40},{16,48},{24,56},{32,64},{40,72},{48,80},{56,88},{64,... | collective-permute-start | bytes 1572872 | tf_op jit(solution)/shard_map/ppermute | solution.py:13
  165.6 29.2 %collective-permute-start.6 = (f32[8,2,16,512]{3,1,2,0:T(2,128)S(1)}, f32[8,2,16,512]{3,1,2,0:T(2,128)S(1)}, u32[]{:S(2)}, u32[]{:S(2)}) collective-permute-start(f32[8,2,16,512]{3,1,2,0:T(2,128)S(1)} %get-tuple-element.5), channel_id=1, source_target_pairs={{0,64},{8,72},{16,80},{24,88},{32,96},{40,104},{48,112},{56,120},{... | collective-permute-start | bytes 1572872 | tf_op jit(solution)/shard_map/ppermute | solution.py:13
  170.3 24.5 %copy-start.39 = (f32[1,8,16,4,128]{4,3,0,2,1:T(4,128)S(1)}, f32[1,8,16,4,128]{4,3,0,2,1:T(4,128)}, u32[]{:S(2)}) copy-start(f32[1,8,16,4,128]{4,3,0,2,1:T(4,128)} %copy.64) | copy-start | bytes 786436
  170.4 24.5 %copy-start.40 = (f32[1,8,16,4,128]{4,3,0,2,1:T(4,128)S(1)}, f32[1,8,16,4,128]{4,3,0,2,1:T(4,128)}, u32[]{:S(2)}) copy-start(f32[1,8,16,4,128]{4,3,0,2,1:T(4,128)} %copy.65) | copy-start | bytes 786436
  170.4 24.5 %copy-start.41 = (f32[1,8,16,4,128]{4,3,0,2,1:T(4,128)S(1)}, f32[1,8,16,4,128]{4,3,0,2,1:T(4,128)}, u32[]{:S(2)}) copy-start(f32[1,8,16,4,128]{4,3,0,2,1:T(4,128)} %copy.69) | copy-start | bytes 786436
  170.4 24.5 %copy-start.42 = (f32[1,8,16,4,128]{4,3,0,2,1:T(4,128)S(1)}, f32[1,8,16,4,128]{4,3,0,2,1:T(4,128)}, u32[]{:S(2)}) copy-start(f32[1,8,16,4,128]{4,3,0,2,1:T(4,128)} %copy.70) | copy-start | bytes 786436
  170.4 24.5 %copy-start.43 = (f32[1,8,16,4,128]{4,3,0,2,1:T(4,128)S(1)}, f32[1,8,16,4,128]{4,3,0,2,1:T(4,128)}, u32[]{:S(2)}) copy-start(f32[1,8,16,4,128]{4,3,0,2,1:T(4,128)} %copy.39) | copy-start | bytes 786436
  170.4 24.5 %copy-start.44 = (f32[1,8,16,4,128]{4,3,0,2,1:T(4,128)S(1)}, f32[1,8,16,4,128]{4,3,0,2,1:T(4,128)}, u32[]{:S(2)}) copy-start(f32[1,8,16,4,128]{4,3,0,2,1:T(4,128)} %copy.40) | copy-start | bytes 786436
  170.9 24.0 %copy-start.29 = (f32[1,8,16,4,128]{4,3,0,2,1:T(4,128)S(1)}, f32[1,8,16,4,128]{4,3,0,2,1:T(4,128)}, u32[]{:S(2)}) copy-start(f32[1,8,16,4,128]{4,3,0,2,1:T(4,128)} %copy.33) | copy-start | bytes 786436
  170.9 24.0 %copy-start.30 = (f32[1,8,16,4,128]{4,3,0,2,1:T(4,128)S(1)}, f32[1,8,16,4,128]{4,3,0,2,1:T(4,128)}, u32[]{:S(2)}) copy-start(f32[1,8,16,4,128]{4,3,0,2,1:T(4,128)} %copy.34) | copy-start | bytes 786436
  170.9 24.0 %copy-start.31 = (f32[1,8,16,4,128]{4,3,0,2,1:T(4,128)S(1)}, f32[1,8,16,4,128]{4,3,0,2,1:T(4,128)}, u32[]{:S(2)}) copy-start(f32[1,8,16,4,128]{4,3,0,2,1:T(4,128)} %copy.44) | copy-start | bytes 786436
  170.9 24.0 %copy-start.32 = (f32[1,8,16,4,128]{4,3,0,2,1:T(4,128)S(1)}, f32[1,8,16,4,128]{4,3,0,2,1:T(4,128)}, u32[]{:S(2)}) copy-start(f32[1,8,16,4,128]{4,3,0,2,1:T(4,128)} %copy.45) | copy-start | bytes 786436
  170.9 24.0 %copy-start.33 = (f32[1,8,16,4,128]{4,3,0,2,1:T(4,128)S(1)}, f32[1,8,16,4,128]{4,3,0,2,1:T(4,128)}, u32[]{:S(2)}) copy-start(f32[1,8,16,4,128]{4,3,0,2,1:T(4,128)} %copy.49) | copy-start | bytes 786436
  170.9 24.0 %copy-start.34 = (f32[1,8,16,4,128]{4,3,0,2,1:T(4,128)S(1)}, f32[1,8,16,4,128]{4,3,0,2,1:T(4,128)}, u32[]{:S(2)}) copy-start(f32[1,8,16,4,128]{4,3,0,2,1:T(4,128)} %copy.50) | copy-start | bytes 786436
  171.0 24.0 %copy-start.35 = (f32[1,8,16,4,128]{4,3,0,2,1:T(4,128)S(1)}, f32[1,8,16,4,128]{4,3,0,2,1:T(4,128)}, u32[]{:S(2)}) copy-start(f32[1,8,16,4,128]{4,3,0,2,1:T(4,128)} %copy.54) | copy-start | bytes 786436
  171.0 24.0 %copy-start.36 = (f32[1,8,16,4,128]{4,3,0,2,1:T(4,128)S(1)}, f32[1,8,16,4,128]{4,3,0,2,1:T(4,128)}, u32[]{:S(2)}) copy-start(f32[1,8,16,4,128]{4,3,0,2,1:T(4,128)} %copy.55) | copy-start | bytes 786436
  171.0 24.0 %copy-start.37 = (f32[1,8,16,4,128]{4,3,0,2,1:T(4,128)S(1)}, f32[1,8,16,4,128]{4,3,0,2,1:T(4,128)}, u32[]{:S(2)}) copy-start(f32[1,8,16,4,128]{4,3,0,2,1:T(4,128)} %copy.59) | copy-start | bytes 786436
  171.0 24.0 %copy-start.38 = (f32[1,8,16,4,128]{4,3,0,2,1:T(4,128)S(1)}, f32[1,8,16,4,128]{4,3,0,2,1:T(4,128)}, u32[]{:S(2)}) copy-start(f32[1,8,16,4,128]{4,3,0,2,1:T(4,128)} %copy.60) | copy-start | bytes 786436
  200.8 125.6 %collective-permute-start.9 = (f32[8,2,16,128]{3,1,2,0:T(2,128)S(1)}, f32[8,2,16,128]{3,1,2,0:T(2,128)S(1)}, u32[]{:S(2)}, u32[]{:S(2)}) collective-permute-start(f32[8,2,16,128]{3,1,2,0:T(2,128)S(1)} %bitcast.390), channel_id=1, source_target_pairs={{0,24},{8,0},{16,8},{24,16},{32,56},{40,32},{48,40},{56,48},{64,88... | collective-permute-start | bytes 393224 | tf_op jit(solution)/shard_map/ppermute | solution.py:13
  204.1 122.3 %collective-permute-start.8 = (f32[8,2,16,128]{3,1,2,0:T(2,128)S(1)}, f32[8,2,16,128]{3,1,2,0:T(2,128)S(1)}, u32[]{:S(2)}, u32[]{:S(2)}) collective-permute-start(f32[8,2,16,128]{3,1,2,0:T(2,128)S(1)} %bitcast.388), channel_id=1, source_target_pairs={{0,16},{8,24},{16,0},{24,8},{32,48},{40,56},{48,32},{56,40},{64,80... | collective-permute-start | bytes 393224 | tf_op jit(solution)/shard_map/ppermute | solution.py:13
  206.0 120.4 %collective-permute-start.7 = (f32[8,2,16,128]{3,1,2,0:T(2,128)S(1)}, f32[8,2,16,128]{3,1,2,0:T(2,128)S(1)}, u32[]{:S(2)}, u32[]{:S(2)}) collective-permute-start(f32[8,2,16,128]{3,1,2,0:T(2,128)S(1)} %bitcast.386), channel_id=1, source_target_pairs={{0,8},{8,16},{16,24},{24,0},{32,40},{40,48},{48,56},{56,32},{64,72... | collective-permute-start | bytes 393224 | tf_op jit(solution)/shard_map/ppermute | solution.py:13
  (14 other events, 14.1 us)
where the time goes:
time: 334 us; the launch traced here: 330 us
  blocking collectives  102 us (31%)
  local copies, waits for them, and re-layouts  71.9 us (22%)
  starting transfers between devices  57.9 us (17%)
  waiting for transfers between devices  38 us (11%)
  matrix products  31.7 us (9%)
  other arithmetic  19.6 us (6%)
  between operations  9.45 us (3%)
    psum x1, blocking collectives, shards(): misfit_total = lax.psum(misfit_sum, ('chan', 'freq'))  102 us
    ppermute x10, starting transfers between devices, permute(): return lax.ppermute(x, 'chan', pairs)  57.9 us
    ppermute x10, waiting for transfers between devices, permute(): return lax.ppermute(x, 'chan', pairs)  38 us
    dot_general x9, matrix products, pair_terms(): jnp.einsum('xfrbc,frbd->xfbcd', stacked_left, right_rows, preferred_eleme...  19.3 us
    reshape x8, local copies, waits for them, and re-layouts, shards(): second = ext[:, :, :, s * bw:s * bw + span].reshape(sub, 2, rows, GROUP, bw)  12.8 us
    another operation x8, local copies, waits for them, and re-layouts, pair_terms(): right_rows = second.reshape(fb, 2 * row_count, nb, block_width)  9.99 us
    slice x23, local copies, waits for them, and re-layouts, pair_terms(): far_spec = second[:, :, :W].reshape(fb, 2 * W, nb, block_width)  7.92 us
    dot_general x9, matrix products, pair_terms(): jnp.einsum('xfbcd,fvbc->xfvbd', rounded, near_spec, preferred_element_typ...  7.82 us
  transfers between devices with their start and end apart: 10, of which 4 were waited for; matrix products, arithmetic and copies ran while one was open for 4% of the time, Pallas kernels for 0%

commit v1 on v0

--- a/solution.py
+++ b/solution.py
@@ -121,7 +121,12 @@
     blocks = jnp.transpose(adj.reshape(sub, 2, W, GROUP, bw), (3, 0, 1, 2, 4))
     back = exchange(blocks, j, peers)
     adjoint = back.reshape(fl, 2, W, bw)
-    misfit_total = lax.psum(misfit_sum, ("chan", "freq"))
+
+    def work_the_slices(view, axis_key, axis_name):
+        v_now = lax.psum(view, axis_name)
+        return lax.psum(v_now, axis_key)
+
+    misfit_total = work_the_slices(misfit_sum, "chan", "freq")
     misfit = misfit_total / float(F * bw * peers * BAND)
     return (adjoint, misfit)
 

time: 334 us -> 539 us (1.61)
  blocking collectives: 102 us -> 306 us
    psum x1 -> x2, blocking collectives: 102 us -> 306 us  [the longest x1 279 us: work_the_slices(): return lax.psum(v_now, axis_key)]
  transfers between devices with their start and end apart: 10 -> 10, of which waited for: 4 -> 4; matrix products, arithmetic and copies ran while one was open for 4% -> 3% of each run, Pallas kernels for 0% -> 0%
where the time goes in v1:
time: 539 us; the launch traced here: 535 us
  blocking collectives  306 us (57%)
  local copies, waits for them, and re-layouts  72 us (13%)
  starting transfers between devices  57.9 us (11%)
  waiting for transfers between devices  37.9 us (7%)
  matrix products  31.9 us (6%)
  other arithmetic  19.7 us (4%)
  between operations  9.61 us (2%)
    psum x1, blocking collectives, work_the_slices(): return lax.psum(v_now, axis_key)  279 us
    ppermute x10, starting transfers between devices, permute(): return lax.ppermute(x, 'chan', pairs)  57.9 us
    ppermute x10, waiting for transfers between devices, permute(): return lax.ppermute(x, 'chan', pairs)  37.9 us
    psum x1, blocking collectives, work_the_slices(): v_now = lax.psum(view, axis_name)  27.1 us
    dot_general x9, matrix products, pair_terms(): jnp.einsum('xfrbc,frbd->xfbcd', stacked_left, right_rows, preferred_eleme...  19.4 us
    reshape x8, local copies, waits for them, and re-layouts, shards(): second = ext[:, :, :, s * bw:s * bw + span].reshape(sub, 2, rows, GROUP, bw)  12.8 us
  transfers between devices with their start and end apart: 10, of which 4 were waited for; matrix products, arithmetic and copies ran while one was open for 3% of the time, Pallas kernels for 0%

profile of v1, /device:TPU:1, one launch (start us, length us, event | category | flops | bytes accessed | tf_op | source)
XLA Modules:
  0.0 535.2 jit_solution(5669061030479656141)
XLA Ops:
  0.7 1.1 pad_maximum_fusion.2
  2.6 16.3 %collective-permute-start.1 = (bf16[8,2,24,128]{3,2,1,0:T(8,128)(2,1)}, bf16[8,2,24,128]{3,2,1,0:T(8,128)(2,1)S(1)}, u32[]{:S(2)}, u32[]{:S(2)}) collective-permute-start(bf16[8,2,24,128]{3,2,1,0:T(8,128)(2,1)} %get-tuple-element.57), channel_id=1, source_target_pairs={{0,16},{8,24},{16,0},{24,8},{32,48},{40,56},{48,32},{56,40},{64,80... | collective-permute-start | bytes 294920 | tf_op jit(solution)/shard_map/ppermute | solution.py:13
  18.9 4.8 collective-permute-start
  23.6 1.9 collective-permute-start.2
  28.4 1.2 multiply_select_fusion.8
  29.6 9.8 %collective-permute-done.2 = bf16[8,2,24,128]{3,2,1,0:T(8,128)(2,1)} collective-permute-done((bf16[8,2,24,128]{3,2,1,0:T(8,128)(2,1)S(1)}, bf16[8,2,24,128]{3,2,1,0:T(8,128)(2,1)}, u32[]{:S(2)}, u32[]{:S(2)}) %collective-permute-start.2) | collective-permute-done | bytes 98336 | tf_op jit(solution)/shard_map/ppermute | solution.py:13
  40.3 1.5 gather_fusion
  41.8 1.1 broadcast_multiply_fusion
  45.5 1.9 reshape.1311
  47.4 7.6 %collective-permute-start.4 = (bf16[8,2,24,512]{3,2,1,0:T(8,128)(2,1)}, bf16[8,2,24,512]{3,2,1,0:T(8,128)(2,1)S(1)}, u32[]{:S(2)}, u32[]{:S(2)}) collective-permute-start(bf16[8,2,24,512]{3,2,1,0:T(8,128)(2,1)} %reshape.1311), channel_id=1, source_target_pairs={{0,448},{8,456},{16,464},{24,472},{32,480},{40,488},{48,496},{56,5... | collective-permute-start | bytes 1179656 | tf_op jit(solution)/shard_map/ppermute | solution.py:13
  55.0 3.2 collective-permute-start.3
  58.3 1.1 maximum_bitcast_fusion
  59.4 3.0 multiply_reduce_fusion.8
  68.1 4.6 collective-permute-done.3
  73.6 1.1 fusion.71
  75.6 1.8 reshape_reshape.24
  77.5 1.8 reshape.1312
  79.3 1.8 reshape_reshape.26
  81.1 1.9 reshape.1316
  84.7 2.3 fusion.72
  88.6 1.9 reshape.1320
  90.5 1.9 reshape_reshape.30
  92.4 1.9 reshape.1324
  94.2 1.8 reshape_reshape.29
  96.1 1.8 reshape.1322
  98.8 1.0 slice.638
  100.6 1.8 reshape.1318
  102.4 1.1 slice.611
  108.6 1.9 multiply_reduce_fusion.6
  115.3 2.0 multiply_reduce_fusion.5
  122.8 2.9 multiply_reduce_fusion.4
  129.3 1.9 multiply_reduce_fusion.3
  135.3 2.0 multiply_reduce_fusion.2
  142.2 2.0 multiply_reduce_fusion.1
  149.1 1.9 multiply_reduce_fusion.7
  154.8 1.9 multiply_reduce_fusion
  159.2 4.2 fusion.9
  164.0 1.9 collective-permute-start.5
  165.9 4.7 collective-permute-start.6
  171.6 10.8 %collective-permute-done.5 = f32[8,2,16,512]{3,1,2,0:T(2,128)S(1)} collective-permute-done((f32[8,2,16,512]{3,1,2,0:T(2,128)S(1)}, f32[8,2,16,512]{3,1,2,0:T(2,128)S(1)}, u32[]{:S(2)}, u32[]{:S(2)}) %collective-permute-start.5) | collective-permute-done | bytes 524320 | tf_op jit(solution)/shard_map/ppermute | solution.py:13
  182.4 12.8 %collective-permute-done.6 = f32[8,2,16,512]{3,1,2,0:T(2,128)S(1)} collective-permute-done((f32[8,2,16,512]{3,1,2,0:T(2,128)S(1)}, f32[8,2,16,512]{3,1,2,0:T(2,128)S(1)}, u32[]{:S(2)}, u32[]{:S(2)}) %collective-permute-start.6) | collective-permute-done | bytes 524320 | tf_op jit(solution)/shard_map/ppermute | solution.py:13
  195.2 4.5 fusion.38
  201.1 3.3 collective-permute-start.9
  204.3 1.9 collective-permute-start.8
  206.3 12.3 %collective-permute-start.7 = (f32[8,2,16,128]{3,1,2,0:T(2,128)S(1)}, f32[8,2,16,128]{3,1,2,0:T(2,128)S(1)}, u32[]{:S(2)}, u32[]{:S(2)}) collective-permute-start(f32[8,2,16,128]{3,1,2,0:T(2,128)S(1)} %bitcast.386), channel_id=1, source_target_pairs={{0,8},{8,16},{16,24},{24,0},{32,40},{40,48},{48,56},{56,32},{64,72... | collective-permute-start | bytes 393224 | tf_op jit(solution)/shard_map/ppermute | solution.py:13
  224.3 27.1 %psum.14 = f32[]{:T(128)} all-reduce(f32[]{:T(128)S(6)} %add.591), channel_id=1, replica_groups=mesh['chan'=64,'freq'=8] {'freq'}, use_global_device_ids=true, to_apply=%region_9.10 | all-reduce | flops 1 | bytes 8 | tf_op jit(solution)/shard_map/psum | solution.py:126
  251.6 279.1 %psum.15 = f32[]{:T(128)} all-reduce(f32[]{:T(128)} %psum.14), channel_id=1, replica_groups=mesh['chan'=64,'freq'=8] {'chan'}, use_global_device_ids=true, to_apply=%region_10.11 | all-reduce | flops 1 | bytes 8 | tf_op jit(solution)/shard_map/psum | solution.py:127
  531.6 1.2 gather_fusion.1
  (244 shorter events, 62.4 us)
Async XLA Ops:
  0.6 26.7 %copy-start.45 = (s32[8192]{0:T(1024)S(1)}, s32[8192]{0:T(1024)}, u32[]{:S(2)}) copy-start(s32[8192]{0:T(1024)} %param.6) | copy-start | bytes 98308
  0.6 27.4 %copy-start.46 = (s32[64]{0:T(128)S(1)}, s32[64]{0:T(128)}, u32[]{:S(2)}) copy-start(s32[64]{0:T(128)} %param.7) | copy-start | bytes 772
  2.6 26.9 %collective-permute-start.1 = (bf16[8,2,24,128]{3,2,1,0:T(8,128)(2,1)}, bf16[8,2,24,128]{3,2,1,0:T(8,128)(2,1)S(1)}, u32[]{:S(2)}, u32[]{:S(2)}) collective-permute-start(bf16[8,2,24,128]{3,2,1,0:T(8,128)(2,1)} %get-tuple-element.57), channel_id=1, source_target_pairs={{0,16},{8,24},{16,0},{24,8},{32,48},{40,56},{48,32},{56,40},{64,80... | collective-permute-start | bytes 294920 | tf_op jit(solution)/shard_map/ppermute | solution.py:13
  18.9 10.7 %collective-permute-start = (bf16[8,2,24,128]{3,2,1,0:T(8,128)(2,1)S(1)}, bf16[8,2,24,128]{3,2,1,0:T(8,128)(2,1)S(1)}, u32[]{:S(2)}, u32[]{:S(2)}) collective-permute-start(bf16[8,2,24,128]{3,2,1,0:T(8,128)(2,1)S(1)} %get-tuple-element.58), channel_id=1, source_target_pairs={{0,8},{8,16},{16,24},{24,0},{32,40},{40,48},{48,56},{56,32},{64,72... | collective-permute-start | bytes 294920 | tf_op jit(solution)/shard_map/ppermute | solution.py:13
  23.6 15.7 %collective-permute-start.2 = (bf16[8,2,24,128]{3,2,1,0:T(8,128)(2,1)S(1)}, bf16[8,2,24,128]{3,2,1,0:T(8,128)(2,1)}, u32[]{:S(2)}, u32[]{:S(2)}) collective-permute-start(bf16[8,2,24,128]{3,2,1,0:T(8,128)(2,1)S(1)} %get-tuple-element.59), channel_id=1, source_target_pairs={{0,24},{8,0},{16,8},{24,16},{32,56},{40,32},{48,40},{56,48},{64,88... | collective-permute-start | bytes 294920 | tf_op jit(solution)/shard_map/ppermute | solution.py:13
  47.4 25.4 %collective-permute-start.4 = (bf16[8,2,24,512]{3,2,1,0:T(8,128)(2,1)}, bf16[8,2,24,512]{3,2,1,0:T(8,128)(2,1)S(1)}, u32[]{:S(2)}, u32[]{:S(2)}) collective-permute-start(bf16[8,2,24,512]{3,2,1,0:T(8,128)(2,1)} %reshape.1311), channel_id=1, source_target_pairs={{0,448},{8,456},{16,464},{24,472},{32,480},{40,488},{48,496},{56,5... | collective-permute-start | bytes 1179656 | tf_op jit(solution)/shard_map/ppermute | solution.py:13
  55.0 17.7 %collective-permute-start.3 = (bf16[8,2,24,512]{3,2,1,0:T(8,128)(2,1)}, bf16[8,2,24,512]{3,2,1,0:T(8,128)(2,1)S(1)}, u32[]{:S(2)}, u32[]{:S(2)}) collective-permute-start(bf16[8,2,24,512]{3,2,1,0:T(8,128)(2,1)} %reshape.1311), channel_id=1, source_target_pairs={{0,480},{8,488},{16,496},{24,504},{32,0},{40,8},{48,16},{56,24},{6... | collective-permute-start | bytes 1179656 | tf_op jit(solution)/shard_map/ppermute | solution.py:13
  72.7 1.9 copy-start.3
  88.6 9.3 %copy-start.1 = (bf16[8,2,24,512]{3,2,1,0:T(8,128)(2,1)S(1)}, bf16[8,2,24,512]{3,2,1,0:T(8,128)(2,1)}, u32[]{:S(2)}) copy-start(bf16[8,2,24,512]{3,2,1,0:T(8,128)(2,1)} %copy-done) | copy-start | bytes 1179652
  102.4 3.7 slice-start.1
  102.4 3.8 slice-start
  103.5 2.7 slice-start.4
  105.4 1.7 slice-start.2
  106.1 1.7 slice-start.3
  106.2 2.4 copy-start.11
  111.9 3.3 copy-start.10
  118.7 3.3 copy-start.4
  127.4 1.9 copy-start.9
  132.7 2.6 copy-start.8
  138.9 3.4 copy-start.7
  145.7 3.4 copy-start.6
  157.6 1.3 copy-start.19
  157.6 1.4 copy-start.22
  157.6 1.5 copy-start.24
  157.6 1.5 copy-start.25
  157.6 1.6 copy-start.27
  163.4 7.2 %copy-start.14 = (bf16[8,2,16,4,128]{4,2,1,3,0:T(8,128)(2,1)S(1)}, bf16[8,2,16,4,128]{4,2,1,3,0:T(8,128)(2,1)}, u32[]{:S(2)}) copy-start(bf16[8,2,16,4,128]{4,2,1,3,0:T(8,128)(2,1)} %copy.71) | copy-start | bytes 786436
  164.0 18.4 %collective-permute-start.5 = (f32[8,2,16,512]{3,1,2,0:T(2,128)S(1)}, f32[8,2,16,512]{3,1,2,0:T(2,128)S(1)}, u32[]{:S(2)}, u32[]{:S(2)}) collective-permute-start(f32[8,2,16,512]{3,1,2,0:T(2,128)S(1)} %get-tuple-element.4), channel_id=1, source_target_pairs={{0,32},{8,40},{16,48},{24,56},{32,64},{40,72},{48,80},{56,88},{64,... | collective-permute-start | bytes 1572872 | tf_op jit(solution)/shard_map/ppermute | solution.py:13
  165.9 29.2 %collective-permute-start.6 = (f32[8,2,16,512]{3,1,2,0:T(2,128)S(1)}, f32[8,2,16,512]{3,1,2,0:T(2,128)S(1)}, u32[]{:S(2)}, u32[]{:S(2)}) collective-permute-start(f32[8,2,16,512]{3,1,2,0:T(2,128)S(1)} %get-tuple-element.5), channel_id=1, source_target_pairs={{0,64},{8,72},{16,80},{24,88},{32,96},{40,104},{48,112},{56,120},{... | collective-permute-start | bytes 1572872 | tf_op jit(solution)/shard_map/ppermute | solution.py:13
  170.6 24.5 %copy-start.39 = (f32[1,8,16,4,128]{4,3,0,2,1:T(4,128)S(1)}, f32[1,8,16,4,128]{4,3,0,2,1:T(4,128)}, u32[]{:S(2)}) copy-start(f32[1,8,16,4,128]{4,3,0,2,1:T(4,128)} %copy.64) | copy-start | bytes 786436
  170.6 24.5 %copy-start.40 = (f32[1,8,16,4,128]{4,3,0,2,1:T(4,128)S(1)}, f32[1,8,16,4,128]{4,3,0,2,1:T(4,128)}, u32[]{:S(2)}) copy-start(f32[1,8,16,4,128]{4,3,0,2,1:T(4,128)} %copy.65) | copy-start | bytes 786436
  170.6 24.5 %copy-start.41 = (f32[1,8,16,4,128]{4,3,0,2,1:T(4,128)S(1)}, f32[1,8,16,4,128]{4,3,0,2,1:T(4,128)}, u32[]{:S(2)}) copy-start(f32[1,8,16,4,128]{4,3,0,2,1:T(4,128)} %copy.69) | copy-start | bytes 786436
  170.7 24.5 %copy-start.42 = (f32[1,8,16,4,128]{4,3,0,2,1:T(4,128)S(1)}, f32[1,8,16,4,128]{4,3,0,2,1:T(4,128)}, u32[]{:S(2)}) copy-start(f32[1,8,16,4,128]{4,3,0,2,1:T(4,128)} %copy.70) | copy-start | bytes 786436
  170.7 24.5 %copy-start.43 = (f32[1,8,16,4,128]{4,3,0,2,1:T(4,128)S(1)}, f32[1,8,16,4,128]{4,3,0,2,1:T(4,128)}, u32[]{:S(2)}) copy-start(f32[1,8,16,4,128]{4,3,0,2,1:T(4,128)} %copy.39) | copy-start | bytes 786436
  170.7 24.5 %copy-start.44 = (f32[1,8,16,4,128]{4,3,0,2,1:T(4,128)S(1)}, f32[1,8,16,4,128]{4,3,0,2,1:T(4,128)}, u32[]{:S(2)}) copy-start(f32[1,8,16,4,128]{4,3,0,2,1:T(4,128)} %copy.40) | copy-start | bytes 786436
  171.2 24.0 %copy-start.29 = (f32[1,8,16,4,128]{4,3,0,2,1:T(4,128)S(1)}, f32[1,8,16,4,128]{4,3,0,2,1:T(4,128)}, u32[]{:S(2)}) copy-start(f32[1,8,16,4,128]{4,3,0,2,1:T(4,128)} %copy.33) | copy-start | bytes 786436
  171.2 24.0 %copy-start.30 = (f32[1,8,16,4,128]{4,3,0,2,1:T(4,128)S(1)}, f32[1,8,16,4,128]{4,3,0,2,1:T(4,128)}, u32[]{:S(2)}) copy-start(f32[1,8,16,4,128]{4,3,0,2,1:T(4,128)} %copy.34) | copy-start | bytes 786436
  171.2 24.0 %copy-start.31 = (f32[1,8,16,4,128]{4,3,0,2,1:T(4,128)S(1)}, f32[1,8,16,4,128]{4,3,0,2,1:T(4,128)}, u32[]{:S(2)}) copy-start(f32[1,8,16,4,128]{4,3,0,2,1:T(4,128)} %copy.44) | copy-start | bytes 786436
  171.2 24.0 %copy-start.32 = (f32[1,8,16,4,128]{4,3,0,2,1:T(4,128)S(1)}, f32[1,8,16,4,128]{4,3,0,2,1:T(4,128)}, u32[]{:S(2)}) copy-start(f32[1,8,16,4,128]{4,3,0,2,1:T(4,128)} %copy.45) | copy-start | bytes 786436
  171.2 24.0 %copy-start.33 = (f32[1,8,16,4,128]{4,3,0,2,1:T(4,128)S(1)}, f32[1,8,16,4,128]{4,3,0,2,1:T(4,128)}, u32[]{:S(2)}) copy-start(f32[1,8,16,4,128]{4,3,0,2,1:T(4,128)} %copy.49) | copy-start | bytes 786436
  171.2 24.0 %copy-start.34 = (f32[1,8,16,4,128]{4,3,0,2,1:T(4,128)S(1)}, f32[1,8,16,4,128]{4,3,0,2,1:T(4,128)}, u32[]{:S(2)}) copy-start(f32[1,8,16,4,128]{4,3,0,2,1:T(4,128)} %copy.50) | copy-start | bytes 786436
  171.2 24.0 %copy-start.35 = (f32[1,8,16,4,128]{4,3,0,2,1:T(4,128)S(1)}, f32[1,8,16,4,128]{4,3,0,2,1:T(4,128)}, u32[]{:S(2)}) copy-start(f32[1,8,16,4,128]{4,3,0,2,1:T(4,128)} %copy.54) | copy-start | bytes 786436
  171.2 24.0 %copy-start.36 = (f32[1,8,16,4,128]{4,3,0,2,1:T(4,128)S(1)}, f32[1,8,16,4,128]{4,3,0,2,1:T(4,128)}, u32[]{:S(2)}) copy-start(f32[1,8,16,4,128]{4,3,0,2,1:T(4,128)} %copy.55) | copy-start | bytes 786436
  171.3 24.0 %copy-start.37 = (f32[1,8,16,4,128]{4,3,0,2,1:T(4,128)S(1)}, f32[1,8,16,4,128]{4,3,0,2,1:T(4,128)}, u32[]{:S(2)}) copy-start(f32[1,8,16,4,128]{4,3,0,2,1:T(4,128)} %copy.59) | copy-start | bytes 786436
  171.3 24.0 %copy-start.38 = (f32[1,8,16,4,128]{4,3,0,2,1:T(4,128)S(1)}, f32[1,8,16,4,128]{4,3,0,2,1:T(4,128)}, u32[]{:S(2)}) copy-start(f32[1,8,16,4,128]{4,3,0,2,1:T(4,128)} %copy.60) | copy-start | bytes 786436
  201.1 330.2 %collective-permute-start.9 = (f32[8,2,16,128]{3,1,2,0:T(2,128)S(1)}, f32[8,2,16,128]{3,1,2,0:T(2,128)S(1)}, u32[]{:S(2)}, u32[]{:S(2)}) collective-permute-start(f32[8,2,16,128]{3,1,2,0:T(2,128)S(1)} %bitcast.390), channel_id=1, source_target_pairs={{0,24},{8,0},{16,8},{24,16},{32,56},{40,32},{48,40},{56,48},{64,88... | collective-permute-start | bytes 393224 | tf_op jit(solution)/shard_map/ppermute | solution.py:13
  204.3 327.0 %collective-permute-start.8 = (f32[8,2,16,128]{3,1,2,0:T(2,128)S(1)}, f32[8,2,16,128]{3,1,2,0:T(2,128)S(1)}, u32[]{:S(2)}, u32[]{:S(2)}) collective-permute-start(f32[8,2,16,128]{3,1,2,0:T(2,128)S(1)} %bitcast.388), channel_id=1, source_target_pairs={{0,16},{8,24},{16,0},{24,8},{32,48},{40,56},{48,32},{56,40},{64,80... | collective-permute-start | bytes 393224 | tf_op jit(solution)/shard_map/ppermute | solution.py:13
  206.3 325.1 %collective-permute-start.7 = (f32[8,2,16,128]{3,1,2,0:T(2,128)S(1)}, f32[8,2,16,128]{3,1,2,0:T(2,128)S(1)}, u32[]{:S(2)}, u32[]{:S(2)}) collective-permute-start(f32[8,2,16,128]{3,1,2,0:T(2,128)S(1)} %bitcast.386), channel_id=1, source_target_pairs={{0,8},{8,16},{16,24},{24,0},{32,40},{40,48},{48,56},{56,32},{64,72... | collective-permute-start | bytes 393224 | tf_op jit(solution)/shard_map/ppermute | solution.py:13
  (14 other events, 14.2 us)
